TPU v7x, 256 devices: a whole 4x4x8 slice. The times are simulated.
256 devices in a mesh: tok: 64 (over x, z, core), ch: 4 (over y).
Axes of the slice: x: 4, y: 4, z: 8, core: 2. Of those that a mesh axis runs over, the one named last changes fastest.
Arguments:
- inputs: float32 [65536, 1024], P('tok', 'ch'), may hold values from -6 to 6
- factor_one: float32 [512, 512], replicated, may hold values from -0.25 to 0.25
- twiddle: float32 [128, 512], P('tok'), may hold values from -4 to 4
- factor_two: float32 [128, 128], replicated, may hold values from -0.5 to 0.5
- w_up: bfloat16 [4, 256, 1024], P('ch', 'tok'), may hold values from -0.375 to 0.375
- w_down: bfloat16 [4, 1024, 256], P('ch', 'tok'), may hold values from -0.1875 to 0.1875
- out_cotangent: float32 [65536, 1024], P('tok', 'ch'), may hold values from -6 to 6
Outputs:
- outputs: float32 [65536, 1024], P('tok', 'ch')
- grad_inputs: float32 [65536, 1024], P('tok', 'ch')
- grad_factor_one: float32 [512, 512], replicated
- grad_factor_two: float32 [128, 128], replicated
- grad_up: float32 [4, 256, 1024], P('ch', 'tok')
- grad_down: float32 [4, 1024, 256], P('ch', 'tok')
All inputs are finite; a program needn't handle non-finite values.
Results may differ from a plain program's by a relative error of at most 0.0057.
Values may be sent and summed in bfloat16 or wider, within the bound.
A program may use at most 64 MiB of HBM per device.

v0:
```python
import math
import jax
import jax.numpy as jnp
from jax import lax
from jax.sharding import PartitionSpec as P

inv_root_two = 1.0 / math.sqrt(2.0)
inv_root_tau = 1.0 / math.sqrt(2.0 * math.pi)


def gelu_parts(value):
    cdf = 0.5 * (1.0 + jax.scipy.special.erf(value * inv_root_two))
    return (value * cdf, cdf + value * jnp.exp(-0.5 * value * value) * inv_root_tau)


def to_columns(block):
    count = lax.axis_size("tok")
    rows, width, chans = block.shape
    return lax.all_to_all(
        block.reshape(rows, count, width // count, chans),
        "tok",
        split_axis=1,
        concat_axis=0,
        tiled=True,
    ).reshape(count * rows, width // count, chans)


def to_rows(block):
    return lax.all_to_all(block, "tok", split_axis=0, concat_axis=1, tiled=True)


def local(inputs, factor_one, twiddle, factor_two, w_up, w_down, out_cotangent):
    high = lax.Precision.HIGHEST
    rows = twiddle.shape[0]
    width = twiddle.shape[1]
    chans = inputs.shape[1]
    panels = (
        lax.all_gather(w_up, "tok", axis=1, tiled=True),
        lax.all_gather(w_down, "tok", axis=1, tiled=True),
    )
    up_w = panels[0][0]
    down_w = panels[1][0]
    grid = inputs.reshape(rows, width, chans)
    first = jnp.einsum("kj,ijc->ikc", factor_one, grid, precision=high)
    mid = first * twiddle[:, :, None]
    mid_cols = to_columns(mid)
    mixed_cols = jnp.einsum("mi,ikc->mkc", factor_two, mid_cols, precision=high)
    mixed = to_rows(mixed_cols).reshape(rows * width, chans)
    gate = jax.nn.sigmoid(inputs)
    branch = inputs + gate * mixed
    normed = branch.astype(jnp.bfloat16)
    up = jnp.dot(normed, up_w, preferred_element_type=jnp.float32)
    active, slope = gelu_parts(up)
    hidden = active.astype(jnp.bfloat16)
    outputs = branch + jnp.dot(hidden, down_w, preferred_element_type=jnp.float32)
    cot = out_cotangent.astype(jnp.bfloat16)
    d_hidden = jnp.dot(cot, down_w.T, preferred_element_type=jnp.float32)
    d_up = (d_hidden * slope).astype(jnp.bfloat16)
    d_branch = out_cotangent + jnp.dot(d_up, up_w.T, preferred_element_type=jnp.float32)
    grad_down_part = jnp.dot(hidden.T, cot, preferred_element_type=jnp.float32)
    grad_up_part = jnp.dot(normed.T, d_up, preferred_element_type=jnp.float32)
    grad_up, grad_down = (
        lax.psum_scatter(grad_up_part[None], "tok", scatter_dimension=1, tiled=True),
        lax.psum_scatter(grad_down_part[None], "tok", scatter_dimension=1, tiled=True),
    )
    d_mixed = d_branch * gate
    direct = d_branch * (1.0 + gate * (1.0 - gate) * mixed)
    cot_cols = to_columns(d_mixed.reshape(rows, width, chans))
    d_mid_cols = jnp.einsum("mi,mkc->ikc", factor_two, cot_cols, precision=high)
    two_part = jnp.einsum("mkc,ikc->mi", cot_cols, mid_cols, precision=high)
    d_first = to_rows(d_mid_cols) * twiddle[:, :, None]
    one_part = jnp.einsum("ikc,ijc->kj", d_first, grid, precision=high)
    d_grid = jnp.einsum("kj,ikc->ijc", factor_one, d_first, precision=high)
    grad_inputs = direct + d_grid.reshape(rows * width, chans)
    grad_one, grad_two = lax.psum((one_part, two_part), ("tok", "ch"))
    return (outputs, grad_inputs, grad_one, grad_two, grad_up, grad_down)


def solution(mesh):
    in_specs = (
        P("tok", "ch"),
        P(),
        P("tok", None),
        P(),
        P("ch", "tok", None),
        P("ch", "tok", None),
        P("tok", "ch"),
    )
    out_specs = (
        P("tok", "ch"),
        P("tok", "ch"),
        P(),
        P(),
        P("ch", "tok", None),
        P("ch", "tok", None),
    )
    return jax.shard_map(local, mesh=mesh, in_specs=in_specs, out_specs=out_specs, check_vma=False)
```

profile of v0, /device:TPU:4, one launch (start us, length us, event | category | flops | bytes accessed | tf_op | source)
XLA Modules:
  0.0 719.0 jit_solution(10194359381156684317)
XLA Ops:
  8.0 0.0 copy-start
  8.0 1.2 copy-done
  9.2 0.0 copy-start.9
  9.2 4.7 fusion.6
  14.0 0.3 copy.65
  14.3 0.1 copy.66
  14.5 0.0 copy-start.12
  14.5 38.7 %all_to_all.63 = f32[2,64,8,256]{3,2,0,1:T(8,128)S(1)} all-to-all(f32[2,64,8,256]{3,2,0,1:T(8,128)S(1)} %copy.66), channel_id=1, replica_groups=mesh['tok'=64,'ch'=4] {'tok'}, dimensions={1} | all-to-all | bytes 2097152 | tf_op jit(solution)/shard_map/all_to_all | solution.py:19
  53.1 1.0 copy-done.4
  54.1 0.0 copy-done.9
  54.1 1.9 convolution_bitcast_fusion.5
  56.0 0.0 copy-start.1
  56.0 1.4 copy.68
  57.4 8.1 %all-to-all-start.1 = ((f32[128,8,256]{2,1,0:T(8,128)}), f32[128,8,256]{2,1,0:T(8,128)S(1)}, u32[]{:S(2)}, u32[]{:S(2)}) async-start(f32[128,8,256]{2,1,0:T(8,128)} %copy.68), calls=%async_computation.1 | async-start | bytes 2097152 | tf_op jit(solution)/shard_map/all_to_all | solution.py:29
  65.5 0.0 copy-done.12
  65.6 72.8 %all_gather.6 = bf16[1,256,1024]{2,0,1:T(2,128)(2,1)} all-gather(bf16[1,4,1024]{2,0,1:T(2,128)(2,1)S(1)} %copy.70), channel_id=1, replica_groups=mesh['tok'=64,'ch'=4] {'tok'}, dimensions={1}, use_global_device_ids=true | all-gather | bytes 532480 | tf_op jit(solution)/shard_map/all_gather | solution.py:38
  138.4 0.0 copy-done.11
  138.4 53.1 %all_gather.7 = bf16[1,1024,256]{2,1,0:T(8,128)(2,1)} all-gather(bf16[1,16,256]{2,1,0:T(8,128)(2,1)S(1)} %copy-done.11), channel_id=1, replica_groups=mesh['tok'=64,'ch'=4] {'tok'}, dimensions={1}, use_global_device_ids=true | all-gather | bytes 532480 | tf_op jit(solution)/shard_map/all_gather | solution.py:39
  191.5 0.0 all-to-all-done.1
  191.5 0.1 copy.69
  191.6 0.0 copy-start.2
  191.6 1.0 copy-done.2
  192.5 0.0 copy-done.1
  192.5 0.3 fusion.11
  192.8 0.2 copy-done.6
  193.1 2.4 multiply_convert_fusion
  195.4 0.0 copy-done.8
  195.4 0.0 copy-done.13
  195.4 2.2 fusion.5
  197.6 0.0 copy-start.7
  197.6 1.8 fusion.33
  199.4 0.0 copy-done.7
  199.4 0.1 copy.71
  199.5 35.5 %all_to_all.64 = f32[2,64,8,256]{3,2,0,1:T(8,128)S(1)} all-to-all(f32[2,64,8,256]{3,2,0,1:T(8,128)S(1)} %copy.71), channel_id=1, replica_groups=mesh['tok'=64,'ch'=4] {'tok'}, dimensions={1} | all-to-all | bytes 2097152 | tf_op jit(solution)/shard_map/all_to_all | solution.py:19
  235.1 1.1 copy-done.5
  236.1 2.9 convolution_bitcast_fusion.4
  239.0 2.7 copy.73
  241.7 8.3 %all-to-all-start.3 = ((f32[128,8,256]{2,1,0:T(8,128)}), f32[128,8,256]{2,1,0:T(8,128)}, u32[]{:S(2)}, u32[]{:S(2)}) async-start(f32[128,8,256]{2,1,0:T(8,128)} %copy.73), calls=%async_computation.3 | async-start | bytes 2097152 | tf_op jit(solution)/shard_map/all_to_all | solution.py:29
  250.0 0.0 all-reduce.5.cloned.1.call-start
  250.0 3.3 convolution_bitcast_fusion.1
  253.3 0.0 all-reduce.5.cloned.1.call-update
  253.4 0.0 reduce-scatter.3.cloned.1.call-start
  253.4 3.6 convolution_bitcast_fusion
  257.0 0.0 reduce-scatter.3.cloned.1.call-update
  257.0 0.3 all-reduce.7.cloned.1.call-start
  257.3 0.0 copy-done.14
  257.3 0.6 dynamic-slice
  258.5 0.0 copy-start.10
  258.6 3.4 convolution_add_fusion.1
  261.9 181.6 %all-reduce.5.cloned.1.call-done = f32[1,256,1024]{2,1,0:T(8,128)} async-done(((f32[1,256,1024]{2,1,0:T(8,128)}), f32[1,256,1024]{2,1,0:T(8,128)}) %all-reduce.5.cloned.1.call-update) | async-done | bytes 1048592
  443.6 1.4 constant_dynamic-slice_fusion
  444.9 3.6 convolution_bitcast_fusion.6
  448.6 0.0 all-to-all-done.3
  448.6 0.0 copy-done.10
  448.6 4.2 convolution_bitcast_fusion.2
  452.8 0.0 all-reduce.7.cloned.1.call-update
  452.8 4.4 convolution_bitcast_fusion.3
  457.2 2.6 copy.76
  459.7 0.0 copy-done.3
  459.7 2.9 fusion.10
  462.7 121.8 %reduce-scatter.3.cloned.1.call-done = f32[1,16,256]{2,1,0:T(8,128)} async-done(((f32[1,1024,256]{2,1,0:T(8,128)}), f32[1,16,256]{2,1,0:T(8,128)}) %reduce-scatter.3.cloned.1.call-update) | async-done | bytes 16400 | tf_op jit(solution)/shard_map/reduce_scatter | solution.py:64
  584.5 123.4 %all-reduce.7.cloned.1.call-done = (f32[512,512]{1,0:T(8,128)}, f32[128,128]{1,0:T(8,128)}) async-done(((f32[512,512]{1,0:T(8,128)}, f32[128,128]{1,0:T(8,128)}), (f32[512,512]{1,0:T(8,128)}, f32[128,128]{1,0:T(8,128)})) %all-reduce.7.cloned.1.call-update) | async-done | bytes 1114128 | tf_op jit(solution)/shard_map/psum | solution.py:75
  707.8 2.3 copy.110
  710.1 1.5 copy.111
  (9 shorter events, 0.0 us)
Async XLA Ops:
  8.0 1.2 copy-start
  9.2 44.9 %copy-start.9 = (f32[128,128]{1,0:T(8,128)S(1)}, f32[128,128]{1,0:T(8,128)}, u32[]{:S(2)}) copy-start(f32[128,128]{1,0:T(8,128)} %param.10) | copy-start | bytes 196612
  14.5 51.1 %copy-start.12 = (bf16[1,4,1024]{2,1,0:T(4,128)(2,1)S(1)}, bf16[1,4,1024]{2,1,0:T(4,128)(2,1)}, u32[]{:S(2)}) copy-start(bf16[1,4,1024]{2,1,0:T(4,128)(2,1)} %param.11) | copy-start | bytes 24580
  53.1 1.0 copy-start.4
  53.1 85.3 %copy-start.11 = (bf16[1,16,256]{2,1,0:T(8,128)(2,1)S(1)}, bf16[1,16,256]{2,1,0:T(8,128)(2,1)}, u32[]{:S(2)}) copy-start(bf16[1,16,256]{2,1,0:T(8,128)(2,1)} %param.12) | copy-start | bytes 24580
  56.0 136.5 %copy-start.1 = (f32[1024,256]{1,0:T(8,128)S(1)}, f32[1024,256]{1,0:T(8,128)}, u32[]{:S(2)}) copy-start(f32[1024,256]{1,0:T(8,128)} %param.7) | copy-start | bytes 3145732
  57.4 134.0 %all-to-all-start.1 = ((f32[128,8,256]{2,1,0:T(8,128)}), f32[128,8,256]{2,1,0:T(8,128)S(1)}, u32[]{:S(2)}, u32[]{:S(2)}) async-start(f32[128,8,256]{2,1,0:T(8,128)} %copy.68), calls=%async_computation.1 | async-start | bytes 2097152 | tf_op jit(solution)/shard_map/all_to_all | solution.py:29
  191.5 1.6 copy-start.6
  191.6 1.0 copy-start.2
  193.1 2.4 copy-start.8
  193.1 2.4 copy-start.13
  197.6 1.8 copy-start.7
  235.1 1.1 copy-start.5
  241.7 206.9 %all-to-all-start.3 = ((f32[128,8,256]{2,1,0:T(8,128)}), f32[128,8,256]{2,1,0:T(8,128)}, u32[]{:S(2)}, u32[]{:S(2)}) async-start(f32[128,8,256]{2,1,0:T(8,128)} %copy.73), calls=%async_computation.3 | async-start | bytes 2097152 | tf_op jit(solution)/shard_map/all_to_all | solution.py:29
  250.0 193.6 %all-reduce.5.cloned.1.call-start = ((), (), s32[]{:S(2)}) async-start(), calls=%async_computation.6 | async-start | bytes 2097152
  253.3 4.0 copy-start.14
  253.4 331.1 %reduce-scatter.3.cloned.1.call-start = ((), (), s32[]{:S(2)}) async-start(), calls=%async_computation.5 | async-start | bytes 1064960 | tf_op jit(solution)/shard_map/reduce_scatter | solution.py:64
  257.0 450.8 %all-reduce.7.cloned.1.call-start = ((), (), s32[]{:S(2)}) async-start(), calls=%async_computation.7 | async-start | bytes 2228224 | tf_op jit(solution)/shard_map/psum | solution.py:75
  258.5 190.0 %copy-start.10 = (f32[2,512]{1,0:T(2,128)S(1)}, f32[2,512]{1,0:T(2,128)}, u32[]{:S(2)}) copy-start(f32[2,512]{1,0:T(2,128)} %param.9) | copy-start | bytes 12292
  448.6 11.2 %copy-start.3 = (f32[2,64,8,256]{3,2,1,0:T(8,128)S(1)}, f32[2,64,8,256]{3,2,1,0:T(8,128)}, u32[]{:S(2)}) copy-start(f32[2,64,8,256]{3,2,1,0:T(8,128)} %copy-done.2) | copy-start | bytes 3145732
Sparse Core Ops, SparseCore 0:
  255.2 188.3 all-reduce.4
  448.1 136.2 reduce-scatter.2
Sparse Core Ops, SparseCore 1:
  452.9 254.9 all-reduce.6
where the time goes:
time: 720 us; the launch traced here: 719 us
  waiting for transfers between devices  427 us (59%)
  blocking collectives  200 us (28%)
  matrix products  38.3 us (5%)
  local copies, waits for them, and re-layouts  17.5 us (2%)
  starting transfers between devices  16.7 us (2%)
  between operations  16.3 us (2%)
    unnamed x4, waiting for transfers between devices  182 us
    psum x1, waiting for transfers between devices, local(): grad_one, grad_two = lax.psum((one_part, two_part), ('tok', 'ch'))  123 us
    reduce_scatter x1, waiting for transfers between devices, local(): lax.psum_scatter(grad_down_part[None], 'tok', scatter_dimension=1, tiled=...  122 us
    all_to_all x2, blocking collectives, to_columns(): lax.all_to_all(block.reshape(rows, count, width // count, chans), 'tok',...  74.2 us
    all_gather x1, blocking collectives, local(): lax.all_gather(w_up, 'tok', axis=1, tiled=True)  72.8 us
    all_gather x1, blocking collectives, local(): lax.all_gather(w_down, 'tok', axis=1, tiled=True)  53.1 us
    all_to_all x2, starting transfers between devices, to_rows(): return lax.all_to_all(block, 'tok', split_axis=0, concat_axis=1, tiled=True)  16.4 us
  transfers between devices with their start and end apart: 5, of which 3 were waited for; matrix products, arithmetic and copies ran while one was open for 4% of the time, Pallas kernels for 0%

commit v1 on v0

--- a/solution.py
+++ b/solution.py
@@ -1,3 +1,4 @@
+import functools
 import math
 import jax
 import jax.numpy as jnp
@@ -6,6 +7,21 @@
 
 inv_root_two = 1.0 / math.sqrt(2.0)
 inv_root_tau = 1.0 / math.sqrt(2.0 * math.pi)
+
+
+def shelves_change(row_data, lane_axis):
+    return jnp.concatenate(
+        lax.all_to_all(
+            jnp.stack([row_data] * lax.axis_size(lane_axis), 0),
+            axis_name=lane_axis,
+            split_axis=0,
+            concat_axis=0,
+        ),
+        1,
+    )
+
+
+scales_solve = functools.partial(shelves_change, lane_axis="tok")
 
 
 def gelu_parts(value):
@@ -34,10 +50,7 @@
     rows = twiddle.shape[0]
     width = twiddle.shape[1]
     chans = inputs.shape[1]
-    panels = (
-        lax.all_gather(w_up, "tok", axis=1, tiled=True),
-        lax.all_gather(w_down, "tok", axis=1, tiled=True),
-    )
+    panels = (scales_solve(w_up), lax.all_gather(w_down, "tok", axis=1, tiled=True))
     up_w = panels[0][0]
     down_w = panels[1][0]
     grid = inputs.reshape(rows, width, chans)

time: 720 us -> 689 us (0.957)
  blocking collectives: 200 us -> 147 us
  waiting for transfers between devices: 427 us -> 440 us
    all_gather x1 -> x0, blocking collectives: 72.8 us -> none  [local(): lax.all_gather(w_up, 'tok', axis=1, tiled=True)]
    all_gather x1, blocking collectives: 53.1 us -> 72.1 us  [local(): lax.all_gather(w_down, 'tok', axis=1, tiled=True)]
    all_to_all x0 -> x1, waiting for transfers between devices: none -> 13.3 us  [shelves_change(): lax.all_to_all(jnp.stack([row_data] * lax.axis_size(lane_axis), 0), axis_...]
    all_to_all x0 -> x1, starting transfers between devices: none -> 8.29 us  [shelves_change(): lax.all_to_all(jnp.stack([row_data] * lax.axis_size(lane_axis), 0), axis_...]
  transfers between devices with their start and end apart: 5 -> 6, of which waited for: 3 -> 4; matrix products, arithmetic and copies ran while one was open for 4% -> 5% of each run, Pallas kernels for 0% -> 0%
where the time goes in v1:
time: 689 us; the launch traced here: 688 us
  waiting for transfers between devices  440 us (64%)
  blocking collectives  147 us (21%)
  matrix products  38.1 us (6%)
  starting transfers between devices  23.8 us (3%)
  local copies, waits for them, and re-layouts  19.3 us (3%)
  between operations  16.4 us (2%)
    unnamed x4, waiting for transfers between devices  182 us
    psum x1, waiting for transfers between devices, local(): grad_one, grad_two = lax.psum((one_part, two_part), ('tok', 'ch'))  123 us
    reduce_scatter x1, waiting for transfers between devices, local(): lax.psum_scatter(grad_down_part[None], 'tok', scatter_dimension=1, tiled=...  122 us
    all_to_all x2, blocking collectives, to_columns(): lax.all_to_all(block.reshape(rows, count, width // count, chans), 'tok',...  74.5 us
    all_gather x1, blocking collectives, local(): lax.all_gather(w_down, 'tok', axis=1, tiled=True)  72.1 us
    all_to_all x2, starting transfers between devices, to_rows(): return lax.all_to_all(block, 'tok', split_axis=0, concat_axis=1, tiled=True)  15.2 us
  transfers between devices with their start and end apart: 6, of which 4 were waited for; matrix products, arithmetic and copies ran while one was open for 5% of the time, Pallas kernels for 0%

profile of v1, /device:TPU:4, one launch (start us, length us, event | category | flops | bytes accessed | tf_op | source)
XLA Modules:
  0.0 687.6 jit_solution(14310546354521418333)
XLA Ops:
  8.0 0.0 copy-start
  8.0 1.2 copy-done
  9.2 4.7 fusion.6
  13.9 0.0 copy-start.9
  14.0 0.3 copy.50
  14.3 0.1 copy.51
  14.4 38.5 %all_to_all.68 = f32[2,64,8,256]{3,2,0,1:T(8,128)S(1)} all-to-all(f32[2,64,8,256]{3,2,0,1:T(8,128)S(1)} %copy.51), channel_id=1, replica_groups=mesh['tok'=64,'ch'=4] {'tok'}, dimensions={1} | all-to-all | bytes 2097152 | tf_op jit(solution)/shard_map/all_to_all | solution.py:35
  53.0 0.0 copy-done.11
  53.0 1.0 stack.2
  54.0 8.3 %all-to-all-start.2 = ((bf16[64,1,4,1024]{3,2,1,0:T(4,128)(2,1)}), bf16[64,1,4,1024]{3,2,1,0:T(4,128)(2,1)}, u32[]{:S(2)}, u32[]{:S(2)}) async-start(bf16[64,1,4,1024]{3,2,1,0:T(4,128)(2,1)} %stack.2), calls=%async_computation.2 | async-start | bytes 1048576 | tf_op jit(solution)/shard_map/all_to_all | solution.py:14
  62.3 0.0 copy-done.4
  62.3 0.0 copy-done.9
  62.4 1.9 convolution_bitcast_fusion.5
  64.3 0.0 copy-start.1
  64.3 1.4 copy.53
  65.7 13.3 %all-to-all-done.2 = bf16[64,1,4,1024]{3,2,1,0:T(4,128)(2,1)} async-done(((bf16[64,1,4,1024]{3,2,1,0:T(4,128)(2,1)}), bf16[64,1,4,1024]{3,2,1,0:T(4,128)(2,1)}, u32[]{:S(2)}, u32[]{:S(2)}) %all-to-all-start.2) | async-done | bytes 524320 | tf_op jit(solution)/shard_map/all_to_all | solution.py:14
  79.0 6.9 %all-to-all-start.1 = ((f32[128,8,256]{2,1,0:T(8,128)}), f32[128,8,256]{2,1,0:T(8,128)S(1)}, u32[]{:S(2)}, u32[]{:S(2)}) async-start(f32[128,8,256]{2,1,0:T(8,128)} %copy.53), calls=%async_computation.1 | async-start | bytes 2097152 | tf_op jit(solution)/shard_map/all_to_all | solution.py:45
  85.9 0.0 copy-done.12
  85.9 72.1 %all_gather.3 = bf16[1,1024,256]{2,1,0:T(8,128)(2,1)} all-gather(bf16[1,16,256]{2,1,0:T(8,128)(2,1)S(1)} %copy-done.12), channel_id=1, replica_groups=mesh['tok'=64,'ch'=4] {'tok'}, dimensions={1}, use_global_device_ids=true | all-gather | bytes 532480 | tf_op jit(solution)/shard_map/all_gather | solution.py:53
  157.9 2.0 squeeze_reshape.3
  159.9 0.0 all-to-all-done.1
  159.9 0.1 copy.54
  160.0 0.0 copy-start.2
  160.0 1.0 copy-done.2
  161.0 0.0 copy-done.1
  161.0 0.3 fusion.11
  161.3 0.0 copy-done.8
  161.3 0.0 copy-start.7
  161.3 0.0 copy-start.13
  161.3 2.2 multiply_convert_fusion
  163.5 0.0 copy-done.7
  163.5 0.0 copy-done.13
  163.5 2.2 fusion.5
  165.6 0.0 copy-start.6
  165.7 1.8 fusion.29
  167.4 0.1 copy.55
  167.5 36.0 %all_to_all.69 = f32[2,64,8,256]{3,2,0,1:T(8,128)S(1)} all-to-all(f32[2,64,8,256]{3,2,0,1:T(8,128)S(1)} %copy.55), channel_id=1, replica_groups=mesh['tok'=64,'ch'=4] {'tok'}, dimensions={1} | all-to-all | bytes 2097152 | tf_op jit(solution)/shard_map/all_to_all | solution.py:35
  203.6 1.1 copy-done.5
  204.6 2.9 convolution_bitcast_fusion.4
  207.5 2.7 copy.57
  210.2 8.3 %all-to-all-start.4 = ((f32[128,8,256]{2,1,0:T(8,128)}), f32[128,8,256]{2,1,0:T(8,128)}, u32[]{:S(2)}, u32[]{:S(2)}) async-start(f32[128,8,256]{2,1,0:T(8,128)} %copy.57), calls=%async_computation.4 | async-start | bytes 2097152 | tf_op jit(solution)/shard_map/all_to_all | solution.py:45
  218.5 0.0 all-reduce.5.cloned.1.call-start
  218.6 3.3 convolution_bitcast_fusion.1
  221.9 0.0 all-reduce.5.cloned.1.call-update
  221.9 0.0 reduce-scatter.3.cloned.1.call-start
  221.9 3.6 convolution_bitcast_fusion
  225.5 0.0 reduce-scatter.3.cloned.1.call-update
  225.6 0.3 all-reduce.7.cloned.1.call-start
  225.8 0.6 dynamic-slice
  227.1 0.0 copy-start.10
  227.1 3.4 convolution_add_fusion.1
  230.4 181.6 %all-reduce.5.cloned.1.call-done = f32[1,256,1024]{2,1,0:T(8,128)} async-done(((f32[1,256,1024]{2,1,0:T(8,128)}), f32[1,256,1024]{2,1,0:T(8,128)}) %all-reduce.5.cloned.1.call-update) | async-done | bytes 1048592
  412.1 1.4 constant_dynamic-slice_fusion
  413.4 3.6 convolution_bitcast_fusion.6
  417.1 0.0 all-to-all-done.4
  417.1 4.2 convolution_bitcast_fusion.2
  421.3 0.0 all-reduce.7.cloned.1.call-update
  421.3 4.4 convolution_bitcast_fusion.3
  425.7 2.6 copy.60
  428.3 2.9 fusion.10
  431.2 121.7 %reduce-scatter.3.cloned.1.call-done = f32[1,16,256]{2,1,0:T(8,128)} async-done(((f32[1,1024,256]{2,1,0:T(8,128)}), f32[1,16,256]{2,1,0:T(8,128)}) %reduce-scatter.3.cloned.1.call-update) | async-done | bytes 16400 | tf_op jit(solution)/shard_map/reduce_scatter | solution.py:77
  552.9 123.5 %all-reduce.7.cloned.1.call-done = (f32[512,512]{1,0:T(8,128)}, f32[128,128]{1,0:T(8,128)}) async-done(((f32[512,512]{1,0:T(8,128)}, f32[128,128]{1,0:T(8,128)}), (f32[512,512]{1,0:T(8,128)}, f32[128,128]{1,0:T(8,128)})) %all-reduce.7.cloned.1.call-update) | async-done | bytes 1114128 | tf_op jit(solution)/shard_map/psum | solution.py:88
  676.4 2.3 copy.81
  678.7 1.5 copy.82
  (11 shorter events, 0.0 us)
Async XLA Ops:
  8.0 1.2 copy-start
  9.2 43.8 %copy-start.11 = (bf16[1,4,1024]{2,1,0:T(4,128)(2,1)S(1)}, bf16[1,4,1024]{2,1,0:T(4,128)(2,1)}, u32[]{:S(2)}) copy-start(bf16[1,4,1024]{2,1,0:T(4,128)(2,1)} %param.11) | copy-start | bytes 24580
  13.9 48.4 %copy-start.9 = (f32[128,128]{1,0:T(8,128)S(1)}, f32[128,128]{1,0:T(8,128)}, u32[]{:S(2)}) copy-start(f32[128,128]{1,0:T(8,128)} %param.10) | copy-start | bytes 196612
  53.0 9.4 %copy-start.4 = (f32[2,64,8,256]{3,2,0,1:T(8,128)}, f32[2,64,8,256]{3,2,0,1:T(8,128)S(1)}, u32[]{:S(2)}) copy-start(f32[2,64,8,256]{3,2,0,1:T(8,128)S(1)} %all_to_all.68) | copy-start | bytes 3145732
  53.0 32.9 %copy-start.12 = (bf16[1,16,256]{2,1,0:T(8,128)(2,1)S(1)}, bf16[1,16,256]{2,1,0:T(8,128)(2,1)}, u32[]{:S(2)}) copy-start(bf16[1,16,256]{2,1,0:T(8,128)(2,1)} %param.12) | copy-start | bytes 24580
  54.0 24.9 %all-to-all-start.2 = ((bf16[64,1,4,1024]{3,2,1,0:T(4,128)(2,1)}), bf16[64,1,4,1024]{3,2,1,0:T(4,128)(2,1)}, u32[]{:S(2)}, u32[]{:S(2)}) async-start(bf16[64,1,4,1024]{3,2,1,0:T(4,128)(2,1)} %stack.2), calls=%async_computation.2 | async-start | bytes 1048576 | tf_op jit(solution)/shard_map/all_to_all | solution.py:14
  64.3 96.7 %copy-start.1 = (f32[1024,256]{1,0:T(8,128)S(1)}, f32[1024,256]{1,0:T(8,128)}, u32[]{:S(2)}) copy-start(f32[1024,256]{1,0:T(8,128)} %param.7) | copy-start | bytes 3145732
  79.0 80.9 %all-to-all-start.1 = ((f32[128,8,256]{2,1,0:T(8,128)}), f32[128,8,256]{2,1,0:T(8,128)S(1)}, u32[]{:S(2)}, u32[]{:S(2)}) async-start(f32[128,8,256]{2,1,0:T(8,128)} %copy.53), calls=%async_computation.1 | async-start | bytes 2097152 | tf_op jit(solution)/shard_map/all_to_all | solution.py:45
  159.9 1.4 copy-start.8
  160.0 1.0 copy-start.2
  161.3 2.2 copy-start.7
  161.3 2.2 copy-start.13
  165.6 1.9 copy-start.6
  203.6 1.1 copy-start.5
  210.2 206.9 %all-to-all-start.4 = ((f32[128,8,256]{2,1,0:T(8,128)}), f32[128,8,256]{2,1,0:T(8,128)}, u32[]{:S(2)}, u32[]{:S(2)}) async-start(f32[128,8,256]{2,1,0:T(8,128)} %copy.57), calls=%async_computation.4 | async-start | bytes 2097152 | tf_op jit(solution)/shard_map/all_to_all | solution.py:45
  218.5 193.6 %all-reduce.5.cloned.1.call-start = ((), (), s32[]{:S(2)}) async-start(), calls=%async_computation.7 | async-start | bytes 2097152
  221.9 4.0 copy-start.14
  221.9 331.0 %reduce-scatter.3.cloned.1.call-start = ((), (), s32[]{:S(2)}) async-start(), calls=%async_computation.6 | async-start | bytes 1064960 | tf_op jit(solution)/shard_map/reduce_scatter | solution.py:77
  225.6 450.9 %all-reduce.7.cloned.1.call-start = ((), (), s32[]{:S(2)}) async-start(), calls=%async_computation.8 | async-start | bytes 2228224 | tf_op jit(solution)/shard_map/psum | solution.py:88
  227.1 190.0 %copy-start.10 = (f32[2,512]{1,0:T(2,128)S(1)}, f32[2,512]{1,0:T(2,128)}, u32[]{:S(2)}) copy-start(f32[2,512]{1,0:T(2,128)} %param.9) | copy-start | bytes 12292
  417.1 11.2 %copy-start.3 = (f32[2,64,8,256]{3,2,1,0:T(8,128)S(1)}, f32[2,64,8,256]{3,2,1,0:T(8,128)}, u32[]{:S(2)}) copy-start(f32[2,64,8,256]{3,2,1,0:T(8,128)} %copy-done.2) | copy-start | bytes 3145732
Sparse Core Ops, SparseCore 0:
  223.7 188.2 all-reduce.4
  416.6 136.2 reduce-scatter.2
Sparse Core Ops, SparseCore 1:
  421.4 254.9 all-reduce.6
